TPU v7x, 32 devices: a whole 2x2x4 slice. The times are simulated.
32 devices in a mesh: seq: 8 (over y, x, core), fsdp: 4 (over z).
Axes of the slice: x: 2, y: 2, z: 4, core: 2. Of those that a mesh axis runs over, the one named last changes fastest.
Arguments:
- block_in: bfloat16 [4096, 1536], P(('seq', 'fsdp')), may hold values from -6 to 6
- norm_gain: float32 [1536], replicated, may hold values from 0.5 to 1.5
- in_weight: bfloat16 [1536, 6448], P('fsdp'), may hold values from -0.15625 to 0.15625
- conv_inner_weight: float32 [4, 48, 64], P(None, 'seq', 'fsdp'), may hold values from -3 to 3
- conv_inner_bias: float32 [48, 64], P('seq', 'fsdp'), may hold values from -3 to 3
- conv_pair_weight: float32 [4, 256], replicated, may hold values from -3 to 3
- conv_pair_bias: float32 [256], replicated, may hold values from -3 to 3
- step_bias: float32 [48], P('seq'), may hold values from -6 to -1
- decay_log: float32 [48], P('seq'), may hold values from 0 to 2.77
- skip_gain: float32 [48], P('seq'), may hold values from 0.5 to 1.5
- gate_gain: float32 [48, 64], P('seq', 'fsdp'), may hold values from 0.5 to 1.5
- out_weight: bfloat16 [3072, 1536], P(None, 'fsdp'), may hold values from -0.109375 to 0.109375
- cotangent: bfloat16 [4096, 1536], P(('seq', 'fsdp')), may hold values from -6 to 6
Outputs:
- block_out: bfloat16 [4096, 1536], P(('seq', 'fsdp'))
- grad_input: bfloat16 [4096, 1536], P(('seq', 'fsdp'))
- grad_norm_gain: float32 [1536], replicated
- grad_in_weight: float32 [1536, 6448], P('fsdp')
- grad_conv_inner_weight: float32 [4, 48, 64], P(None, 'seq', 'fsdp')
- grad_conv_inner_bias: float32 [48, 64], P('seq', 'fsdp')
- grad_conv_pair_weight: float32 [4, 256], replicated
- grad_conv_pair_bias: float32 [256], replicated
- grad_step_bias: float32 [48], P('seq')
- grad_decay_log: float32 [48], P('seq')
- grad_skip_gain: float32 [48], P('seq')
- grad_gate_gain: float32 [48, 64], P('seq', 'fsdp')
- grad_out_weight: float32 [3072, 1536], P(None, 'fsdp')
All inputs are finite; a program needn't handle non-finite values.
Results may differ from a plain program's by a relative error of at most 0.015.
The roundings to bfloat16 on the way count: a program that leaves them out, or rounds other values in their place, can miss the bound.
Values may be sent and summed in bfloat16 or wider, within the bound.
No kernel may reach another device: no remote copies, remote signals or barrier semaphores. Data moves between devices by JAX's collectives and lax.ppermute only.
A program may use at most 384 MiB of HBM per device.

v0:
```python
import jax
import jax.numpy as jnp
from jax import lax
from jax.sharding import PartitionSpec as P

H = 48
P_SIZE = 64
N = 128
KW = 4
Q = 256


norm_epsilon = 1e-05
far_below = -1e30
highest = lax.Precision.HIGHEST


def conv_silu(values, weight, shift_bias):
    length = values.shape[1]
    tap_count = weight.shape[0]
    padded = jnp.pad(values, ((0, 0), (tap_count - 1, 0)))
    summed = shift_bias[:, None] + jnp.zeros_like(values)
    for offset in range(tap_count):
        summed = summed + weight[offset][:, None] * padded[:, offset : offset + length]
    return jax.nn.silu(summed)


def block_step(carry_state, inputs):
    inner_piece, b_piece, c_piece, rate_piece, step_piece, scores = inputs
    block_len = rate_piece.shape[1]
    cumulative = jnp.cumsum(rate_piece, axis=1)
    causal_mask = lax.broadcasted_iota(
        jnp.int32, (block_len, block_len), 0
    ) >= lax.broadcasted_iota(jnp.int32, (block_len, block_len), 1)
    spread = cumulative[:, :, None] - cumulative[:, None, :]
    decay_mask = jnp.exp(jnp.where(causal_mask[None], spread, far_below))
    mixing = scores[None] * decay_mask * step_piece[:, None, :]
    output = jnp.einsum("hpj,hij->hpi", inner_piece, mixing, precision=highest)
    carried = jnp.einsum("hpn,ni->hpi", carry_state, c_piece, precision=highest)
    output = output + carried * jnp.exp(cumulative)[:, None, :]
    tail_weight = jnp.exp(cumulative[:, -1:] - cumulative) * step_piece
    fresh_state = jnp.einsum(
        "hpj,nj->hpn", inner_piece * tail_weight[:, None, :], b_piece, precision=highest
    )
    carry_state = jnp.exp(cumulative[:, -1])[:, None, None] * carry_state + fresh_state
    return (carry_state, output)


def mixer_heads(inner_conv, pair_conv, step_raw, step_bias, decay_log, skip_gain, score_blocks):
    heads_here, width_here, length = inner_conv.shape
    blocks = length // Q
    step_size = jax.nn.softplus(step_raw + step_bias[:, None])
    log_decay = step_size * (-jnp.exp(decay_log))[:, None]
    inner_blocks = jnp.moveaxis(inner_conv.reshape(heads_here, width_here, blocks, Q), 2, 0)
    pair_blocks = jnp.moveaxis(pair_conv.reshape(2 * N, blocks, Q), 1, 0)
    rate_blocks = jnp.moveaxis(log_decay.reshape(heads_here, blocks, Q), 1, 0)
    step_blocks = jnp.moveaxis(step_size.reshape(heads_here, blocks, Q), 1, 0)
    initial = jnp.zeros((heads_here, width_here, N), jnp.float32)
    last_state, outputs = lax.scan(
        jax.checkpoint(block_step),
        initial,
        (
            inner_blocks,
            pair_blocks[:, :N],
            pair_blocks[:, N:],
            rate_blocks,
            step_blocks,
            score_blocks,
        ),
    )
    mixer_out = jnp.moveaxis(outputs, 0, 2).reshape(heads_here, width_here, length)
    return mixer_out + skip_gain[:, None, None] * inner_conv


def body(
    block_in,
    norm_gain,
    in_weight,
    conv_inner_weight,
    conv_inner_bias,
    conv_pair_weight,
    conv_pair_bias,
    step_bias,
    decay_log,
    skip_gain,
    gate_gain,
    out_weight,
    cotangent,
):
    groups_seq = lax.axis_size("seq")
    groups_fsdp = lax.axis_size("fsdp")
    devices = groups_seq * groups_fsdp
    tokens = block_in.shape[0]
    heads_here = decay_log.shape[0]
    width_here = gate_gain.shape[1]
    channels = heads_here * width_here
    inner_width = H * P_SIZE
    length = tokens * devices
    blocks = length // Q
    hidden = block_in.astype(jnp.float32)
    inverse_scale = lax.rsqrt(jnp.mean(hidden * hidden, axis=1, keepdims=True) + norm_epsilon)
    normed = (hidden * inverse_scale * norm_gain[None, :]).astype(jnp.bfloat16)
    in_full, out_full = (
        lax.all_gather(in_weight, "fsdp", axis=0, tiled=True),
        lax.all_gather(out_weight, "fsdp", axis=1, tiled=True),
    )
    proj_columns = in_full.shape[1]
    projected = jnp.dot(normed, in_full, preferred_element_type=jnp.float32).astype(jnp.bfloat16)
    gate_inner = projected[:, : 2 * inner_width].reshape(
        tokens, 2, groups_seq, heads_here, groups_fsdp, width_here
    )
    gate_inner = jnp.transpose(gate_inner, (2, 4, 1, 3, 5, 0)).reshape(
        devices, 2 * channels, tokens
    )
    step_part = projected[:, 2 * inner_width + 2 * N :].reshape(tokens, groups_seq, 1, heads_here)
    step_part = jnp.broadcast_to(step_part, (tokens, groups_seq, groups_fsdp, heads_here))
    step_part = jnp.transpose(step_part, (1, 2, 3, 0)).reshape(devices, heads_here, tokens)
    pair_part = jnp.transpose(projected[:, 2 * inner_width : 2 * inner_width + 2 * N])
    arrived = lax.all_to_all(
        jnp.concatenate([gate_inner, step_part], axis=1),
        ("seq", "fsdp"),
        split_axis=0,
        concat_axis=2,
        tiled=True,
    )[0]
    pair_all = lax.all_gather(pair_part, ("seq", "fsdp"), axis=1, tiled=True)
    inner_act, inner_pull = jax.vjp(
        conv_silu,
        arrived[channels : 2 * channels].astype(jnp.float32),
        conv_inner_weight.reshape(KW, channels),
        conv_inner_bias.reshape(channels),
    )
    inner_conv = lax.optimization_barrier(inner_act.astype(jnp.bfloat16)).astype(jnp.float32)
    pair_act, pair_pull = jax.vjp(
        conv_silu, pair_all.astype(jnp.float32), conv_pair_weight, conv_pair_bias
    )
    pair_low = lax.optimization_barrier(pair_act.astype(jnp.bfloat16))
    pair_conv = pair_low.astype(jnp.float32)
    pair_low_blocks = jnp.moveaxis(pair_low.reshape(2 * N, blocks, Q), 1, 0)
    score_blocks = jnp.einsum(
        "bni,bnj->bij",
        pair_low_blocks[:, N:],
        pair_low_blocks[:, :N],
        preferred_element_type=jnp.float32,
    )
    step_here = arrived[2 * channels :].astype(jnp.float32)
    mixer_out, mixer_pull = jax.vjp(
        mixer_heads,
        inner_conv.reshape(heads_here, width_here, length),
        pair_conv,
        step_here,
        step_bias,
        decay_log,
        skip_gain,
        score_blocks,
    )
    mixer_flat = mixer_out.reshape(channels, length)
    gate_here = arrived[:channels].astype(jnp.float32)
    gate_silu = jax.nn.silu(gate_here)
    gated_out = mixer_flat * gate_silu
    square_sum = lax.psum(jnp.sum(gated_out * gated_out, axis=0), ("seq", "fsdp"))
    gate_scale = lax.rsqrt(square_sum / inner_width + norm_epsilon)
    gain_flat = gate_gain.reshape(channels)
    gated_normed = (gated_out * gate_scale[None, :] * gain_flat[:, None]).astype(jnp.bfloat16)
    returned = lax.all_to_all(
        gated_normed.reshape(channels, devices, tokens),
        ("seq", "fsdp"),
        split_axis=1,
        concat_axis=0,
        tiled=True,
    )
    normed_tokens = jnp.transpose(
        returned.reshape(groups_seq, groups_fsdp, heads_here, width_here, tokens), (0, 2, 1, 3, 4)
    ).reshape(inner_width, tokens)
    branch = lax.dot_general(
        normed_tokens, out_full, (((0,), (0,)), ((), ())), preferred_element_type=jnp.float32
    )
    block_out = (hidden + branch).astype(jnp.bfloat16)
    cotangent_float = cotangent.astype(jnp.float32)
    back_normed = lax.dot_general(
        out_full, cotangent, (((1,), (1,)), ((), ())), preferred_element_type=jnp.float32
    ).astype(jnp.bfloat16)
    back_send = jnp.transpose(
        back_normed.reshape(groups_seq, heads_here, groups_fsdp, width_here, tokens),
        (0, 2, 1, 3, 4),
    ).reshape(devices, channels, tokens)
    back_here = lax.all_to_all(back_send, ("seq", "fsdp"), split_axis=0, concat_axis=2, tiled=True)[
        0
    ].astype(jnp.float32)
    grad_gate_gain = jnp.sum(back_here * gated_out * gate_scale[None, :], axis=1).reshape(
        heads_here, width_here
    )
    back_gain = back_here * gain_flat[:, None]
    cross_sum = lax.psum(jnp.sum(back_gain * gated_out, axis=0), ("seq", "fsdp"))
    scale_cubed = gate_scale * gate_scale * gate_scale
    back_gated = (
        gate_scale[None, :] * back_gain
        - gated_out * (scale_cubed * cross_sum / inner_width)[None, :]
    )
    back_mixer = back_gated * gate_silu
    sigmoid_gate = jax.nn.sigmoid(gate_here)
    back_gate = back_gated * mixer_flat * sigmoid_gate * (1.0 + gate_here * (1.0 - sigmoid_gate))
    (
        back_inner_conv,
        back_pair_direct,
        back_step,
        step_bias_part,
        decay_part,
        skip_part,
        back_scores,
    ) = mixer_pull(back_mixer.reshape(heads_here, width_here, length))
    pair_float_blocks = jnp.moveaxis(pair_conv.reshape(2 * N, blocks, Q), 1, 0)
    back_c_blocks = jnp.einsum(
        "bij,bnj->bni", back_scores, pair_float_blocks[:, :N], precision=highest
    )
    back_b_blocks = jnp.einsum(
        "bij,bni->bnj", back_scores, pair_float_blocks[:, N:], precision=highest
    )
    back_pair_scores = jnp.moveaxis(
        jnp.concatenate([back_b_blocks, back_c_blocks], axis=1), 0, 1
    ).reshape(2 * N, length)
    back_pair_conv = back_pair_direct + back_pair_scores
    back_inner_raw, conv_inner_weight_grad, conv_inner_bias_grad = inner_pull(
        back_inner_conv.reshape(channels, length)
    )
    back_pair_raw, pair_weight_part, pair_bias_part = pair_pull(back_pair_conv)
    tokens_send = (
        jnp.concatenate([back_gate, back_inner_raw], axis=0)
        .astype(jnp.bfloat16)
        .reshape(2 * channels, devices, tokens)
    )
    back_tokens = lax.all_to_all(
        tokens_send, ("seq", "fsdp"), split_axis=1, concat_axis=0, tiled=True
    )
    back_zx = jnp.transpose(
        back_tokens.reshape(groups_seq, groups_fsdp, 2, heads_here, width_here, tokens),
        (2, 0, 3, 1, 4, 5),
    ).reshape(2 * inner_width, tokens)
    head_start = lax.axis_index("seq") * heads_here
    step_full = lax.dynamic_update_slice(
        jnp.zeros((H, length), jnp.float32), back_step, (head_start, 0)
    )
    back_pair_tok, back_step_tok = (
        lax.psum_scatter(back_pair_raw, ("seq", "fsdp"), scatter_dimension=1, tiled=True),
        lax.psum_scatter(step_full, ("seq", "fsdp"), scatter_dimension=1, tiled=True),
    )
    back_all = jnp.concatenate(
        [back_zx, back_pair_tok.astype(jnp.bfloat16), back_step_tok.astype(jnp.bfloat16)], axis=0
    )
    back_normed_in = lax.dot_general(
        back_all, in_full, (((0,), (1,)), ((), ())), preferred_element_type=jnp.float32
    )
    gain_part = jnp.sum(back_normed_in * hidden * inverse_scale, axis=0)
    scaled_back = back_normed_in * norm_gain[None, :]
    inverse_cubed = inverse_scale * inverse_scale * inverse_scale
    grad_input = (
        cotangent_float
        + inverse_scale * scaled_back
        - hidden * inverse_cubed * jnp.mean(scaled_back * hidden, axis=1, keepdims=True)
    ).astype(jnp.bfloat16)
    in_term = lax.dot_general(
        normed, back_all, (((0,), (1,)), ((), ())), preferred_element_type=jnp.float32
    )
    out_term = lax.dot_general(
        cotangent, normed_tokens, (((0,), (1,)), ((), ())), preferred_element_type=jnp.float32
    )
    summed_part = lax.psum_scatter(
        jnp.concatenate([in_term, out_term], axis=1).astype(jnp.bfloat16),
        "fsdp",
        scatter_dimension=0,
        tiled=True,
    )
    owned_rows = lax.psum(summed_part, "seq").astype(jnp.float32)
    grad_in_weight = owned_rows[:, :proj_columns]
    grad_out_weight = jnp.transpose(owned_rows[:, proj_columns:])
    head_parts = lax.dynamic_update_slice(
        jnp.zeros((3, H), jnp.float32),
        jnp.stack([step_bias_part, decay_part, skip_part]),
        (0, head_start),
    )
    head_sums, pair_weight_sum, pair_bias_sum, gain_sum = lax.psum(
        (head_parts, pair_weight_part, pair_bias_part, gain_part), ("seq", "fsdp")
    )
    head_grads = lax.dynamic_slice(head_sums, (0, head_start), (3, heads_here))
    return (
        block_out,
        grad_input,
        gain_sum,
        grad_in_weight,
        conv_inner_weight_grad.reshape(KW, heads_here, width_here),
        conv_inner_bias_grad.reshape(heads_here, width_here),
        pair_weight_sum,
        pair_bias_sum,
        head_grads[0],
        head_grads[1],
        head_grads[2],
        grad_gate_gain,
        grad_out_weight,
    )


def solution(mesh):
    in_specs = (
        P(("seq", "fsdp"), None),
        P(),
        P("fsdp", None),
        P(None, "seq", "fsdp"),
        P("seq", "fsdp"),
        P(),
        P(),
        P("seq"),
        P("seq"),
        P("seq"),
        P("seq", "fsdp"),
        P(None, "fsdp"),
        P(("seq", "fsdp"), None),
    )
    out_specs = (
        P(("seq", "fsdp"), None),
        P(("seq", "fsdp"), None),
        P(),
        P("fsdp", None),
        P(None, "seq", "fsdp"),
        P("seq", "fsdp"),
        P(),
        P(),
        P("seq"),
        P("seq"),
        P("seq"),
        P("seq", "fsdp"),
        P(None, "fsdp"),
    )
    return jax.shard_map(body, mesh=mesh, in_specs=in_specs, out_specs=out_specs, check_vma=False)
```

profile of v0, /device:TPU:0, one launch (start us, length us, event | category | flops | bytes accessed | tf_op | source)
XLA Modules:
  0.0 2372.7 jit_solution(2314175445322762893)
XLA Ops:
  9.6 169.5 %all-gather.8.cloned.1.call-done = bf16[3072,1536]{1,0:T(8,128)(2,1)} async-done(((bf16[3072,384]{1,0:T(8,128)(2,1)}), bf16[3072,1536]{1,0:T(8,128)(2,1)}) %all-gather.8.cloned.1.call-update) | async-done | bytes 9437200 | tf_op jit(solution)/shard_map/all_gather | solution.py:105
  189.2 339.7 %all-gather.4.cloned.1.call-done = bf16[1536,6448]{0,1:T(8,128)(2,1)} async-done(((bf16[384,6448]{0,1:T(8,128)(2,1)}), bf16[1536,6448]{0,1:T(8,128)(2,1)}) %all-gather.4.cloned.1.call-update) | async-done | bytes 19808272 | tf_op jit(solution)/shard_map/all_gather | solution.py:104
  529.0 9.6 convolution_convert_fusion.2
  552.3 35.3 %all-to-all-done = bf16[32,198,128]{2,1,0:T(8,128)(2,1)S(1)} async-done(((bf16[32,198,128]{2,1,0:T(8,128)(2,1)}), bf16[32,198,128]{2,1,0:T(8,128)(2,1)S(1)}, u32[]{:S(2)}, u32[]{:S(2)}) %all-to-all-start) | async-done | bytes 1622048 | tf_op jit(solution)/shard_map/all_to_all | solution.py:119
  599.9 7.8 all-gather.6.cloned.1.call-done
  622.7 177.8 %while.43 = (s32[]{:T(128)}, f32[6,16,128]{2,1,0:T(8,128)S(1)}, f32[16,6,16,256]{3,2,1,0:T(8,128)}, f32[16,6,16,128]{3,2,1,0:T(8,128)}, f32[16,6,256]{2,1,0:T(8,...) while((s32[]{:T(128)}, f32[6,16,128]{2,1,0:T(8,128)S(1)}, ...), condition=%wide.region_4.5_spmd.clone, body=%wide.region_1.4_spmd.clone.sunk | while | flops 152902672 | bytes 1983900 | solution.py:59
  807.2 39.8 %psum.49 = f32[4096]{0:T(1024)S(1)} all-reduce(f32[4096]{0:T(1024)S(1)} %get-tuple-element.830), channel_id=1, replica_groups=mesh['seq'=8,'fsdp'=4] {'seq','fsdp'}, use_global_device_ids=true, to_apply=%region_6.7 | all-reduce | flops 4096 | bytes 32768 | tf_op jit(solution)/shard_map/psum | solution.py:161
  851.2 39.6 %psum.50 = f32[4096]{0:T(1024)S(1)} all-reduce(f32[4096]{0:T(1024)S(1)} %get-tuple-element.752), channel_id=1, replica_groups=mesh['seq'=8,'fsdp'=4] {'seq','fsdp'}, use_global_device_ids=true, to_apply=%region_8.9 | all-reduce | flops 4096 | bytes 32768 | tf_op jit(solution)/shard_map/psum | solution.py:194
  890.8 8.1 multiply_reduce_fusion.8
  908.9 490.8 %while.44 = (s32[]{:T(128)}, f32[6,16,128]{2,1,0:T(8,128)S(1)}, f32[16,6,16,256]{3,2,1,0:T(8,128)}, f32[16,128,256]{2,1,0:T(8,128)}, f32[16,128,256]{2,1,0:T(8,1...) while((s32[]{:T(128)}, f32[6,16,128]{2,1,0:T(8,128)S(1)}, ...), condition=%wide.region_22.23_spmd.clone, body=%wide.region_9.22_spmd.clone.sunk | while | flops 347122208 | bytes 5884363 | solution.py:59
  958.5 7.6 reduce-window.74
  989.2 7.6 reduce-window.74
  1019.8 7.6 reduce-window.74
  1050.5 7.6 reduce-window.74
  1081.2 7.6 reduce-window.74
  1142.5 7.6 reduce-window.74
  1173.2 7.6 reduce-window.74
  1203.9 7.6 reduce-window.74
  1234.6 7.6 reduce-window.74
  1296.0 7.6 reduce-window.74
  1326.7 7.6 reduce-window.74
  1457.0 10.4 all-to-all-done.1
  1472.2 40.8 %reduce-scatter.8.cloned.1.call-done = f32[48,128]{1,0:T(8,128)} async-done(((f32[48,4096]{1,0:T(8,128)}), f32[48,128]{1,0:T(8,128)}) %reduce-scatter.8.cloned.1.call-update) | async-done | bytes 24592 | tf_op jit(solution)/shard_map/reduce_scatter | solution.py:245
  1523.5 140.0 %reduce-scatter.6.cloned.1.call-done = f32[256,128]{1,0:T(8,128)} async-done(((f32[256,4096]{1,0:T(8,128)}), f32[256,128]{1,0:T(8,128)}) %reduce-scatter.6.cloned.1.call-update) | async-done | bytes 131088 | tf_op jit(solution)/shard_map/reduce_scatter | solution.py:244
  1664.4 14.1 convolution_convert_fusion
  1678.6 26.7 %pad_maximum_fusion = bf16[1536,9520]{0,1:T(8,128)(2,1)} fusion(bf16[1536,3072]{0,1:T(8,128)(2,1)} %fusion.81, bf16[1536,6448]{0,1:T(8,128)(2,1)} %convolution_convert_fusion), kind=kLoop, calls=%fused_computation.109 | loop fusion | flops 58490880 | bytes 58490880 | tf_op jit(solution)/shard_map/concatenate | solution.py:268
  1705.3 35.6 %copy.204 = bf16[1536,9520]{1,0:T(8,128)(2,1)} copy(bf16[1536,9520]{0,1:T(8,128)(2,1)} %pad_maximum_fusion) | data formatting | bytes 58490880
  1740.9 482.8 %reduce-scatter.10.cloned.1.call-done = bf16[384,9520]{1,0:T(8,128)(2,1)} async-done(((bf16[1536,9520]{1,0:T(8,128)(2,1)}), bf16[384,9520]{1,0:T(8,128)(2,1)}) %reduce-scatter.10.cloned.1.call-update) | async-done | bytes 7311376
  2223.7 10.6 copy.205
  2248.2 10.1 fusion.114
  2258.4 42.4 %all-reduce.22 = (f32[1536]{0:T(1024)}, f32[4,256]{1,0:T(4,128)}, f32[256]{0:T(256)}, f32[3,48]{1,0:T(4,128)S(1)}) all-reduce(f32[1536]{0:T(1024)S(1)} %get-tuple-element.758, f32[4,256]{1,0:T(4,128)S(1)} %pad_add_fusion.6, f32[256]{0:T(256)S(1)} %copy-done.69, ...), channel_id=1, replica_groups=mesh['seq'=8,'fsdp'=4] {'seq','fsdp'}, use_global_device_ids=true, to_apply=%region_27.28 | all-reduce | flops 2960 | bytes 23680 | tf_op jit(solution)/shard_map/psum | solution.py:281
  2302.5 50.1 %all-reduce.25.cloned.1.call-done = bf16[384,9520]{0,1:T(8,128)(2,1)} async-done(((bf16[384,9520]{0,1:T(8,128)(2,1)}), bf16[384,9520]{0,1:T(8,128)(2,1)}) %all-reduce.25.cloned.1.call-update) | async-done | bytes 7311376 | tf_op jit(solution)/shard_map/psum | solution.py:273
  (1471 shorter events, 758.7 us)
Async XLA Ops:
  7.2 171.9 %all-gather.8.cloned.1.call-start = ((), (), s32[]{:S(2)}) async-start(), calls=%async_computation.9 | async-start | bytes 11796480 | tf_op jit(solution)/shard_map/all_gather | solution.py:105
  7.9 171.2 %copy-start.27 = (bf16[128,1536]{1,0:T(8,128)(2,1)S(1)}, bf16[128,1536]{1,0:T(8,128)(2,1)}, u32[]{:S(2)}) copy-start(bf16[128,1536]{1,0:T(8,128)(2,1)} %param.29) | copy-start | bytes 1179652
  7.9 521.0 %all-gather.4.cloned.1.call-start = ((), (), s32[]{:S(2)}) async-start(), calls=%async_computation.7 | async-start | bytes 24760320 | tf_op jit(solution)/shard_map/all_gather | solution.py:104
  9.6 519.3 %copy-start.41 = (f32[128]{0:T(128)}, f32[128]{0:T(128)S(1)}, u32[]{:S(2)}) copy-start(f32[128]{0:T(128)S(1)} %get-tuple-element.876) | copy-start | bytes 1540
  185.4 343.6 %copy-start.36 = (f32[1536]{0:T(1024)S(1)}, f32[1536]{0:T(1024)}, u32[]{:S(2)}) copy-start(f32[1536]{0:T(1024)} %param.18) | copy-start | bytes 18436
  186.4 355.2 %all-to-all-start.2 = ((bf16[32,96,128]{2,1,0:T(8,128)(2,1)}), bf16[32,96,128]{2,1,0:T(8,128)(2,1)S(1)}, u32[]{:S(2)}, u32[]{:S(2)}) async-start(bf16[32,96,128]{2,1,0:T(8,128)(2,1)} %bitcast.25), calls=%async_computation.2 | async-start | bytes 1572864 | tf_op jit(solution)/shard_map/all_to_all | solution.py:187
  542.5 45.0 %all-to-all-start = ((bf16[32,198,128]{2,1,0:T(8,128)(2,1)}), bf16[32,198,128]{2,1,0:T(8,128)(2,1)S(1)}, u32[]{:S(2)}, u32[]{:S(2)}) async-start(bf16[32,198,128]{2,1,0:T(8,128)(2,1)} %pad_maximum_fusion.2), calls=%async_computation | async-start | bytes 3276800 | tf_op jit(solution)/shard_map/all_to_all | solution.py:119
  546.2 61.5 %all-gather.6.cloned.1.call-start = ((), (), s32[]{:S(2)}) async-start(), calls=%async_computation.8 | async-start | bytes 2162688 | tf_op jit(solution)/shard_map/all_gather | solution.py:126
  547.7 965.3 %reduce-scatter.8.cloned.1.call-start = ((), (), s32[]{:S(2)}) async-start(), calls=%async_computation.11 | async-start | bytes 811008 | tf_op jit(solution)/shard_map/reduce_scatter | solution.py:245
  548.1 42.9 %copy-start.58 = (f32[96]{0:T(128)}, f32[96]{0:T(128)S(1)}, u32[]{:S(2)}) copy-start(f32[96]{0:T(128)S(1)} %mul.764) | copy-start | bytes 1156
  548.2 42.8 %copy-start.60 = (f32[96]{0:T(128)}, f32[96]{0:T(128)S(1)}, u32[]{:S(2)}) copy-start(f32[96]{0:T(128)S(1)} %mul.761) | copy-start | bytes 1156
  548.3 42.8 %copy-start.62 = (f32[96]{0:T(128)}, f32[96]{0:T(128)S(1)}, u32[]{:S(2)}) copy-start(f32[96]{0:T(128)S(1)} %mul.758) | copy-start | bytes 1156
  548.4 42.7 %copy-start.64 = (f32[96]{0:T(128)}, f32[96]{0:T(128)S(1)}, u32[]{:S(2)}) copy-start(f32[96]{0:T(128)S(1)} %mul.755) | copy-start | bytes 1156
  548.6 342.2 %copy-start.52 = (f32[96]{0:T(128)}, f32[96]{0:T(128)S(1)}, u32[]{:S(2)}) copy-start(f32[96]{0:T(128)S(1)} %mul.782) | copy-start | bytes 1156
  548.7 47.0 %copy-start.56 = (f32[6]{0:T(128)}, f32[6]{0:T(128)S(1)}, u32[]{:S(2)}) copy-start(f32[6]{0:T(128)S(1)} %exponential_negate_fusion) | copy-start | bytes 76
  548.8 61.0 %copy-start.44 = (f32[1,256]{1,0:T(1,128)}, f32[1,256]{1,0:T(1,128)S(1)}, u32[]{:S(2)}) copy-start(f32[1,256]{1,0:T(1,128)S(1)} %get-tuple-element.868) | copy-start | bytes 3076
  548.8 61.0 %copy-start.46 = (f32[1,256]{1,0:T(1,128)}, f32[1,256]{1,0:T(1,128)S(1)}, u32[]{:S(2)}) copy-start(f32[1,256]{1,0:T(1,128)S(1)} %get-tuple-element.869) | copy-start | bytes 3076
  548.8 61.0 %copy-start.48 = (f32[1,256]{1,0:T(1,128)}, f32[1,256]{1,0:T(1,128)S(1)}, u32[]{:S(2)}) copy-start(f32[1,256]{1,0:T(1,128)S(1)} %get-tuple-element.870) | copy-start | bytes 3076
  548.8 61.0 %copy-start.50 = (f32[1,256]{1,0:T(1,128)}, f32[1,256]{1,0:T(1,128)S(1)}, u32[]{:S(2)}) copy-start(f32[1,256]{1,0:T(1,128)S(1)} %get-tuple-element.871) | copy-start | bytes 3076
  1168.3 14.3 copy-start.39
  1321.8 14.3 copy-start.39
  1321.8 14.3 copy-start.40
  1412.8 250.7 %reduce-scatter.6.cloned.1.call-start = ((), (), s32[]{:S(2)}) async-start(), calls=%async_computation.10 | async-start | bytes 4325376 | tf_op jit(solution)/shard_map/reduce_scatter | solution.py:244
  1442.8 24.7 %all-to-all-start.1 = ((bf16[96,32,128]{2,0,1:T(8,128)(2,1)}), bf16[96,32,128]{2,0,1:T(8,128)(2,1)S(1)}, u32[]{:S(2)}, u32[]{:S(2)}) async-start(bf16[96,32,128]{2,0,1:T(8,128)(2,1)} %bitcast.450), calls=%async_computation.1 | async-start | bytes 1572864 | tf_op jit(solution)/shard_map/all_to_all | solution.py:165
  1457.0 58.1 %copy-start.28 = (bf16[128,1536]{1,0:T(8,128)(2,1)S(1)}, bf16[128,1536]{1,0:T(8,128)(2,1)}, u32[]{:S(2)}) copy-start(bf16[128,1536]{1,0:T(8,128)(2,1)} %param.29) | copy-start | bytes 1179652
  1467.5 46.3 %copy-start.23 = (bf16[96,32,128]{2,0,1:T(8,128)(2,1)}, bf16[96,32,128]{2,0,1:T(8,128)(2,1)S(1)}, u32[]{:S(2)}) copy-start(bf16[96,32,128]{2,0,1:T(8,128)(2,1)S(1)} %all-to-all-done.1) | copy-start | bytes 2359300
  1467.5 52.9 %all-to-all-start.3 = ((bf16[192,32,128]{2,0,1:T(8,128)(2,1)}), bf16[192,32,128]{2,0,1:T(8,128)(2,1)S(1)}, u32[]{:S(2)}, u32[]{:S(2)}) async-start(bf16[192,32,128]{2,0,1:T(8,128)(2,1)} %pad_maximum_fusion.3), calls=%async_computation.3 | async-start | bytes 3145728 | tf_op jit(solution)/shard_map/all_to_all | solution.py:232
  1472.1 751.6 %reduce-scatter.10.cloned.1.call-start = ((), (), s32[]{:S(2)}) async-start(), calls=%async_computation.13 | async-start | bytes 36864000
  1521.6 142.9 %copy-start.37 = (f32[1536]{0:T(1024)S(1)}, f32[1536]{0:T(1024)}, u32[]{:S(2)}) copy-start(f32[1536]{0:T(1024)} %param.18) | copy-start | bytes 18436
  1521.6 142.9 %copy-start.42 = (f32[128]{0:T(128)S(1)}, f32[128]{0:T(128)}, u32[]{:S(2)}) copy-start(f32[128]{0:T(128)} %copy-done.41) | copy-start | bytes 1540
  1740.9 611.7 %all-reduce.25.cloned.1.call-start = ((), (), s32[]{:S(2)}) async-start(), calls=%async_computation.12 | async-start | bytes 14622720 | tf_op jit(solution)/shard_map/psum | solution.py:273
  2248.2 53.1 %copy-start.73 = (f32[128]{0:T(128)S(1)}, f32[128]{0:T(128)}, u32[]{:S(2)}) copy-start(f32[128]{0:T(128)} %get-tuple-element.875) | copy-start | bytes 1540
  (144 other events, 989.7 us)
Sparse Core Ops, SparseCore 0:
  9.6 169.4 all-gather.7
  180.7 348.2 all-gather.3
  550.4 57.2 all-gather.5
  1412.9 100.0 reduce-scatter.7
  1515.1 148.3 reduce-scatter.5
  1741.0 482.6 reduce-scatter.9
  2234.4 118.1 all-reduce.24
where the time goes:
time: 2390 us; the launch traced here: 2370 us
  waiting for transfers between devices  1280 us (54%)
  other arithmetic  317 us (13%)
  local copies, waits for them, and re-layouts  316 us (13%)
  matrix products  306 us (13%)
  blocking collectives  122 us (5%)
    unnamed x8, waiting for transfers between devices  484 us
    all_gather x1, waiting for transfers between devices, body(): lax.all_gather(in_weight, 'fsdp', axis=0, tiled=True)  340 us
    another operation x128, other arithmetic  183 us
    all_gather x1, waiting for transfers between devices, body(): lax.all_gather(out_weight, 'fsdp', axis=1, tiled=True)  169 us
    dot_general x48, matrix products, block_step(): output = jnp.einsum('hpj,hij->hpi', inner_piece, mixing, precision=highest)  161 us
    reduce_scatter x1, waiting for transfers between devices, body(): lax.psum_scatter(back_pair_raw, ('seq', 'fsdp'), scatter_dimension=1, til...  140 us
    squeeze x80, local copies, waits for them, and re-layouts, mixer_heads(): lax.scan(jax.checkpoint(block_step), initial, (inner_blocks, pair_blocks[...  81.6 us
    unnamed x151, local copies, waits for them, and re-layouts  67.4 us
  transfers between devices with their start and end apart: 11, of which 9 were waited for; matrix products, arithmetic and copies ran while one was open for 4% of the time, Pallas kernels for 0%

commit v1 on v0

v1 whole, which is shorter than its diff:
```python
import jax
import jax.numpy as jnp
from jax import lax
from jax.sharding import PartitionSpec as P

H = 48
P_SIZE = 64
N = 128
KW = 4
Q = 256

norm_epsilon = 1e-05
far_below = -1e30
highest = lax.Precision.HIGHEST
f32 = jnp.float32
bf16 = jnp.bfloat16
everyone = ("seq", "fsdp")


def spread(value, axis, count, groups=None):
    copies = jnp.broadcast_to(value[None], (count,) + value.shape)
    return lax.all_to_all(copies, axis, 0, 0, axis_index_groups=groups, tiled=True)


def dot_f32(left, right, dims, batch=((), ())):
    return lax.dot_general(left, right, (dims, batch), preferred_element_type=f32)


def body(
    block_in,
    norm_gain,
    in_weight,
    conv_inner_weight,
    conv_inner_bias,
    conv_pair_weight,
    conv_pair_bias,
    step_bias,
    decay_log,
    skip_gain,
    gate_gain,
    out_weight,
    cotangent,
):
    S = lax.axis_size("seq")
    F = lax.axis_size("fsdp")
    devices = S * F
    R = S // F
    s = lax.axis_index("seq")
    f = lax.axis_index("fsdp")
    q = s // R
    c = s % R
    member = c * F + f
    tokens, D = block_in.shape
    TL = tokens * S
    blocks = TL // Q
    HG = H // S
    GW = HG * P_SIZE
    QW = GW // F
    DI = H * P_SIZE
    Dl = in_weight.shape[0]
    PF = P_SIZE // F
    PQ = 2 * N // F
    parts = [[cc + R * qq for qq in range(F)] for cc in range(R)]
    twins = [(i, i ^ 1) for i in range(S)]
    forth = [(i, i + R) for i in range(S - R)]
    back = [(i + R, i) for i in range(S - R)]

    def twin(value):
        return lax.ppermute(value, "seq", twins)

    def pair_up(value):
        other = twin(value)
        return jnp.where(
            c == 0, jnp.stack([value, other]), jnp.stack([other, value])
        )

    def gather_group(value):
        line = spread(value, "fsdp", F)
        return pair_up(line).reshape((S * value.shape[0],) + value.shape[1:])

    def scatter_group(value):
        halves = value.reshape(R, F * tokens, value.shape[1])
        away = jnp.where(c == 0, halves[1], halves[0])
        mine = jnp.where(c == 0, halves[0], halves[1])
        total = mine.astype(f32) + twin(away.astype(bf16)).astype(f32)
        sent = total.astype(bf16).reshape(F, tokens, value.shape[1])
        got = lax.all_to_all(sent, "fsdp", 0, 0, tiled=True)
        return jnp.sum(got.astype(f32), axis=0)

    small = jnp.concatenate(
        [
            conv_inner_weight.reshape(KW, HG * PF),
            conv_inner_bias.reshape(1, HG * PF),
            gate_gain.reshape(1, HG * PF),
        ],
        axis=0,
    )
    small = jnp.pad(small, ((0, 0), (0, 128 - HG * PF)))
    heads_row = jnp.concatenate([step_bias, decay_log, skip_gain])
    heads_row = jnp.pad(heads_row, (0, 128 - 3 * HG))[None]
    small = jnp.concatenate([small, heads_row, jnp.zeros((1, 128), f32)], axis=0)
    small_all = spread(small, everyone, devices)
    small_here = lax.dynamic_slice(small_all, (member * F, 0, 0), (F, 8, 128))
    chan = small_here[:, : KW + 2, : HG * PF].reshape(F, KW + 2, HG, PF)
    chan = jnp.transpose(chan, (1, 2, 0, 3)).reshape(KW + 2, GW)
    heads_here = small_here[0, KW + 2]
    bias_h = heads_here[:HG]
    rate_h = jnp.exp(heads_here[HG : 2 * HG])
    skip_h = heads_here[2 * HG : 3 * HG]
    gain_row = chan[KW + 1]
    conv_w = jnp.concatenate([chan[:KW], conv_pair_weight], axis=1)
    conv_b = jnp.concatenate([chan[KW], conv_pair_bias])

    def head_rows(columns):
        half = lax.dynamic_slice(columns, (0, c * (DI // R)), (Dl, DI // R))
        rows = jnp.transpose(half).reshape(F, F, QW, Dl)
        return lax.dynamic_slice(rows, (0, q, 0, 0), (F, 1, QW, Dl)).reshape(F, QW, Dl)

    pair_rows = jnp.transpose(in_weight[:, 2 * DI : 2 * DI + 2 * N]).reshape(F, PQ, Dl)
    pair_rows = lax.dynamic_slice(pair_rows, (q, 0, 0), (1, PQ, Dl))
    pair_rows = jnp.broadcast_to(pair_rows, (F, PQ, Dl))
    step_rows = jnp.transpose(in_weight[:, 2 * DI + 2 * N :]).reshape(R, F, HG, Dl)
    step_rows = lax.dynamic_slice(step_rows, (c, 0, 0, 0), (1, F, HG, Dl)).reshape(F, HG, Dl)
    step_rows = jnp.pad(step_rows, ((0, 0), (0, 8 - HG), (0, 0)))
    sent = jnp.concatenate(
        [
            head_rows(in_weight[:, :DI]),
            head_rows(in_weight[:, DI : 2 * DI]),
            pair_rows,
            step_rows,
        ],
        axis=1,
    )
    got = lax.all_to_all(sent, "fsdp", 0, 0, tiled=True)
    rows = jnp.transpose(got, (1, 0, 2)).reshape(2 * QW + PQ + 8, D)
    rows = spread(rows, "seq", F, parts)
    in_rows = jnp.concatenate(
        [
            rows[:, :QW].reshape(GW, D),
            rows[:, QW : 2 * QW].reshape(GW, D),
            rows[0, 2 * QW + PQ :],
        ],
        axis=0,
    )
    pair_in = rows[:, 2 * QW : 2 * QW + PQ].reshape(2 * N, D)

    out_sent = lax.dynamic_slice(
        out_weight.reshape(R, F, F, QW, Dl), (c, 0, q, 0, 0), (1, F, 1, QW, Dl)
    ).reshape(F, QW, Dl)
    out_got = lax.all_to_all(out_sent, "fsdp", 0, 0, tiled=True)
    out_rows = jnp.transpose(out_got, (1, 0, 2)).reshape(QW, D)
    out_rows = spread(out_rows, "seq", F, parts).reshape(GW, D)

    hidden = block_in.astype(f32)
    inverse_scale = lax.rsqrt(jnp.mean(hidden * hidden, axis=1, keepdims=True) + norm_epsilon)
    normed = (hidden * inverse_scale * norm_gain[None, :]).astype(bf16)
    x_group = gather_group(normed)
    cot_group = gather_group(cotangent)

    proj = dot_f32(x_group, in_rows, ((1,), (1,))).astype(bf16)
    pair_raw = dot_f32(x_group, pair_in, ((1,), (1,))).astype(bf16)
    gate = proj[:, :GW].astype(f32)
    raw = jnp.concatenate([proj[:, GW : 2 * GW], pair_raw], axis=1)
    halo = lax.ppermute(raw[TL - (KW - 1) :], "seq", forth)
    step_raw = proj[:, 2 * GW : 2 * GW + HG].astype(f32)

    raw_ext = jnp.concatenate([halo, raw], axis=0).astype(f32)
    pre = conv_b[None] + sum(
        conv_w[k][None] * raw_ext[k : k + TL] for k in range(KW)
    )
    sig_pre = jax.nn.sigmoid(pre)
    act = lax.optimization_barrier((pre * sig_pre).astype(bf16))
    act_slope = sig_pre * (1.0 + pre * (1.0 - sig_pre))
    xs = act[:, :GW].reshape(blocks, Q, HG, P_SIZE)
    bs = act[:, GW : GW + N].reshape(blocks, Q, N)
    cs = act[:, GW + N :].reshape(blocks, Q, N)

    step_in = step_raw + bias_h[None]
    step = jax.nn.softplus(step_in)
    log_decay = step * (-rate_h)[None]
    causal = lax.broadcasted_iota(jnp.int32, (Q, Q), 0) >= lax.broadcasted_iota(
        jnp.int32, (Q, Q), 1
    )
    lower = causal.astype(f32)
    ld = log_decay.reshape(blocks, Q, HG)
    dt = step.reshape(blocks, Q, HG)
    cum = jnp.einsum("ij,bjh->bih", lower, ld, precision=highest)
    total = cum[:, -1]
    tail = jnp.exp(total[:, None] - cum)
    head = jnp.exp(cum)
    xf = xs.astype(f32)
    u32 = xf * dt[..., None]
    u = lax.optimization_barrier(u32.astype(bf16))
    uw = (u32 * tail[..., None]).astype(bf16)
    scores = jnp.einsum("bin,bjn->bij", cs, bs, preferred_element_type=f32)
    cum_t = jnp.transpose(cum, (0, 2, 1))
    decay = jnp.exp(
        jnp.where(causal[None, None], cum_t[:, :, :, None] - cum_t[:, :, None, :], far_below)
    )
    mix = lax.optimization_barrier((scores[:, None] * decay).astype(bf16))

    def wide(per_head):
        return jnp.repeat(per_head, P_SIZE, axis=-1)

    fresh = jnp.einsum(
        "bjn,bjw->bnw", bs, uw.reshape(blocks, Q, GW), preferred_element_type=f32
    )
    local = [jnp.zeros((N, GW), f32)]
    for b in range(blocks):
        local.append(local[b] * wide(jnp.exp(total[b]))[None] + fresh[b])
    whole_total = jnp.sum(total, axis=0)
    packed = jnp.concatenate(
        [local[blocks], jnp.broadcast_to(wide(whole_total)[None], (8, GW))], axis=0
    )
    packed = spread(packed, "seq", F, parts)
    totals = packed[:, N, :]
    part_no = jnp.arange(F)
    before = jnp.zeros((N, GW), f32)
    for p in range(F):
        between = jnp.sum(jnp.where(((part_no > p) & (part_no < q))[:, None], totals, 0.0), axis=0)
        before = before + jnp.where(p < q, jnp.exp(between)[None] * packed[p, :N], 0.0)
    prefix = jnp.cumsum(total, axis=0) - total
    states = jnp.stack(
        [local[b] + wide(jnp.exp(prefix[b]))[None] * before for b in range(blocks)]
    )
    states_low = states.astype(bf16)
    y_intra = jnp.einsum("bhij,bjhp->bihp", mix, u, preferred_element_type=f32)
    carried = jnp.einsum("bin,bnw->biw", cs, states_low, preferred_element_type=f32)
    y_inter = carried.reshape(blocks, Q, HG, P_SIZE) * head[..., None]
    mixer = y_intra + y_inter + skip_h[:, None] * xf
    mixer_flat = mixer.reshape(TL, GW)
    sig = jax.nn.sigmoid(gate)
    silu_gate = gate * sig
    gated = mixer_flat * silu_gate

    back_normed = dot_f32(cot_group, out_rows, ((1,), (1,))).astype(bf16).astype(f32)
    back_gain = back_normed * gain_row[None]
    sums = jnp.stack([jnp.sum(gated * gated, axis=1), jnp.sum(back_gain * gated, axis=1)])
    sums = sums + twin(sums)
    sums = jnp.sum(spread(sums, "fsdp", F), axis=0)
    scale = lax.rsqrt(sums[0] / DI + norm_epsilon)[:, None]
    cross = (sums[1][:, None] * scale * scale * scale) / DI
    gated_normed = (gated * scale * gain_row[None]).astype(bf16)
    branch = scatter_group(dot_f32(gated_normed, out_rows, ((1,), (0,))))
    block_out = (hidden + branch).astype(bf16)
    gate_gain_part = jnp.sum(back_normed * gated * scale, axis=0)
    back_gated = scale * back_gain - gated * cross
    back_mixer = back_gated * silu_gate
    back_gate = (back_gated * mixer_flat * sig * (1.0 + gate * (1.0 - sig))).astype(bf16)

    def finish_in(part):
        rows4 = part.astype(bf16).reshape(F, F, Dl // F, GW)
        got = lax.all_to_all(
            jnp.transpose(rows4, (1, 0, 2, 3)), "seq", 0, 0, axis_index_groups=parts, tiled=True
        )
        mine = jnp.sum(got.astype(f32), axis=0).astype(bf16)
        cols = lax.all_to_all(mine, "fsdp", 0, 0, tiled=True)
        everywhere = spread(cols, "seq", F, parts)
        full = pair_up(everywhere)
        return jnp.transpose(full, (1, 3, 0, 2, 4)).reshape(Dl, DI).astype(f32)

    def finish_out(part):
        got = lax.all_to_all(
            part.astype(bf16).reshape(F, QW, D),
            "seq",
            0,
            0,
            axis_index_groups=parts,
            tiled=True,
        )
        mine = jnp.sum(got.astype(f32), axis=0).astype(bf16).reshape(QW, F, Dl)
        cols = lax.all_to_all(jnp.transpose(mine, (1, 0, 2)), "fsdp", 0, 0, tiled=True)
        everywhere = spread(cols, "seq", F, parts)
        full = pair_up(everywhere)
        return jnp.transpose(full, (0, 2, 1, 3, 4)).reshape(DI, Dl).astype(f32)

    grad_out_weight = finish_out(dot_f32(gated_normed, cot_group, ((0,), (0,))))
    grad_gate_cols = finish_in(dot_f32(x_group, back_gate, ((0,), (0,))))

    dy = back_mixer.reshape(blocks, Q, HG, P_SIZE)
    dy_low = lax.optimization_barrier(dy.astype(bf16))
    dyh = (dy * head[..., None]).astype(bf16).reshape(blocks, Q, GW)
    fresh_back = jnp.einsum("bin,biw->bnw", cs, dyh, preferred_element_type=f32)
    local_back = [jnp.zeros((N, GW), f32)]
    for b in reversed(range(blocks)):
        local_back.append(local_back[-1] * wide(jnp.exp(total[b]))[None] + fresh_back[b])
    local_back = local_back[::-1]
    packed_back = spread(local_back[0], "seq", F, parts)
    after = jnp.zeros((N, GW), f32)
    for p in range(F):
        between = jnp.sum(jnp.where(((part_no < p) & (part_no > q))[:, None], totals, 0.0), axis=0)
        after = after + jnp.where(p > q, jnp.exp(between)[None] * packed_back[p], 0.0)
    suffix = whole_total[None] - prefix - total
    states_back = jnp.stack(
        [
            local_back[b + 1] + wide(jnp.exp(suffix[b]))[None] * after
            for b in range(blocks)
        ]
    )
    back_low = states_back.astype(bf16)
    back_mix = jnp.einsum("bihp,bjhp->bhij", dy_low, u, preferred_element_type=f32)
    back_scores = jnp.sum(back_mix * decay, axis=1).astype(bf16)
    back_c = jnp.einsum("bij,bjn->bin", back_scores, bs, preferred_element_type=f32)
    back_c = back_c + jnp.einsum("biw,bnw->bin", dyh, states_low, preferred_element_type=f32)
    back_b = jnp.einsum("bij,bin->bjn", back_scores, cs, preferred_element_type=f32)
    back_b = back_b + jnp.einsum(
        "bjw,bnw->bjn", uw.reshape(blocks, Q, GW), back_low, preferred_element_type=f32
    )
    du_intra = jnp.einsum("bhij,bihp->bjhp", mix, dy_low, preferred_element_type=f32)
    du_inter = (
        jnp.einsum("bjn,bnw->bjw", bs, back_low, preferred_element_type=f32).reshape(
            blocks, Q, HG, P_SIZE
        )
        * tail[..., None]
    )
    du = du_intra + du_inter
    back_x = du * dt[..., None] + skip_h[:, None] * dy
    back_dt = jnp.sum(xf * du, axis=-1)
    row_term = jnp.sum(dy_low.astype(f32) * y_intra + dy * y_inter, axis=-1)
    col_intra = jnp.sum(u.astype(f32) * du_intra, axis=-1)
    col_inter = jnp.sum(u32 * du_inter, axis=-1)
    across = jnp.sum(
        (states_back * states).reshape(blocks, N, HG, P_SIZE), axis=(1, 3)
    ) * jnp.exp(total)
    strict = lower - jnp.eye(Q, dtype=f32)
    back_ld = (
        jnp.einsum("it,bih->bth", lower, row_term - col_intra, precision=highest)
        + jnp.einsum("tj,bjh->bth", strict, col_inter, precision=highest)
        + across[:, None]
    ).reshape(TL, HG)
    back_dt = back_dt.reshape(TL, HG) - rate_h[None] * back_ld
    back_step = back_dt * jax.nn.sigmoid(step_in)
    step_bias_part = jnp.sum(back_step, axis=0)
    decay_part = jnp.sum(back_ld * log_decay, axis=0)
    skip_part = jnp.sum((dy * xf).reshape(TL, HG, P_SIZE), axis=(0, 2))

    back_act = jnp.concatenate(
        [back_x.reshape(TL, GW), back_b.reshape(TL, N), back_c.reshape(TL, N)], axis=1
    )
    back_pre = back_act * act_slope
    halo_back = lax.ppermute(back_pre[: KW - 1], "seq", back)
    back_ext = jnp.concatenate([back_pre, halo_back], axis=0)
    back_raw = sum(
        conv_w[k][None] * back_ext[KW - 1 - k : KW - 1 - k + TL] for k in range(KW)
    )
    conv_w_part = jnp.stack(
        [jnp.sum(back_pre * raw_ext[k : k + TL], axis=0) for k in range(KW)]
    )
    conv_b_part = jnp.sum(back_pre, axis=0)
    back_inner = back_raw[:, :GW].astype(bf16)
    back_pair_own = scatter_group(back_raw[:, GW:]).astype(bf16)
    back_step_low = back_step.astype(bf16)

    rows_low = jnp.concatenate(
        [back_gate, back_inner, jnp.pad(back_step_low, ((0, 0), (0, 8 - HG)))], axis=1
    )
    back_in = scatter_group(dot_f32(rows_low, in_rows, ((1,), (0,))))
    back_in = back_in + dot_f32(back_pair_own, pair_in, ((1,), (0,)))
    gain_part = jnp.sum(back_in * hidden * inverse_scale, axis=0)
    scaled_back = back_in * norm_gain[None, :]
    inverse_cubed = inverse_scale * inverse_scale * inverse_scale
    grad_input = (
        cotangent.astype(f32)
        + inverse_scale * scaled_back
        - hidden * inverse_cubed * jnp.mean(scaled_back * hidden, axis=1, keepdims=True)
    ).astype(bf16)

    grad_inner_cols = finish_in(dot_f32(x_group, back_inner, ((0,), (0,))))
    step_wide = jnp.pad(jnp.transpose(back_step_low), ((0, 8 - HG), (0, 0)))
    step_wide = step_wide.reshape(8 * TL // (2 * N), 2 * N)
    rest = pair_up(spread(jnp.concatenate([back_pair_own, step_wide], axis=0), "fsdp", F))
    rest = rest.reshape(S, tokens + step_wide.shape[0], 2 * N)
    pair_all = rest[:, :tokens].reshape(TL, 2 * N)
    step_all = rest[:, tokens:].reshape(S, 8, TL)[:, :HG].reshape(H, TL)
    x_rows = lax.dynamic_slice(x_group, (0, f * Dl), (TL, Dl))
    grad_pair = dot_f32(x_rows, pair_all, ((0,), (0,)))
    grad_step = dot_f32(step_all, x_rows, ((1,), (0,)))
    grad_rest = jnp.concatenate([jnp.transpose(grad_pair), grad_step], axis=0).astype(bf16)
    grad_rest = jnp.sum(spread(grad_rest, "seq", F, parts).astype(f32), axis=0)
    grad_in_weight = jnp.concatenate(
        [grad_gate_cols, grad_inner_cols, jnp.transpose(grad_rest)], axis=1
    )

    per_channel = jnp.concatenate(
        [conv_w_part[:, :GW], conv_b_part[None, :GW], gate_gain_part[None]], axis=0
    )
    per_channel = jnp.transpose(per_channel.reshape(KW + 2, HG, F, PF), (2, 0, 1, 3))
    per_channel = jnp.pad(
        per_channel.reshape(F, KW + 2, HG * PF), ((0, 0), (0, 0), (0, 128 - HG * PF))
    )
    per_head = jnp.concatenate([step_bias_part, decay_part, skip_part])
    per_head = jnp.broadcast_to(jnp.pad(per_head, (0, 128 - 3 * HG))[None, None], (F, 1, 128))
    slots = lax.dynamic_update_slice(
        jnp.zeros((devices, KW + 3, 128), f32),
        jnp.concatenate([per_channel, per_head], axis=1),
        (member * F, 0, 0),
    )
    pair_grads = jnp.concatenate([conv_w_part[:, GW:], conv_b_part[None, GW:]], axis=0)
    shared = jnp.concatenate(
        [
            pair_grads.reshape(devices, (KW + 1) * 2 * N // devices),
            gain_part.reshape(devices, D // devices),
        ],
        axis=1,
    )
    width = shared.shape[1]
    shared = jnp.pad(shared, ((0, 0), (0, 128 - width)))[:, None]
    slots = jnp.concatenate([slots, shared], axis=1)
    mine = jnp.sum(lax.all_to_all(slots, everyone, 0, 0, tiled=True), axis=0)
    shared_all = spread(mine[KW + 3 :], everyone, devices)[:, 0]
    cut = (KW + 1) * 2 * N // devices
    pair_grads = shared_all[:, :cut].reshape(KW + 1, 2 * N)
    gain_sum = shared_all[:, cut:width].reshape(D)
    channel_grads = mine[: KW + 2, : HG * PF].reshape(KW + 2, HG, PF)
    head_grads = mine[KW + 2]
    return (
        block_out,
        grad_input,
        gain_sum,
        grad_in_weight,
        channel_grads[:KW],
        channel_grads[KW],
        pair_grads[:KW],
        pair_grads[KW],
        head_grads[:HG],
        head_grads[HG : 2 * HG],
        head_grads[2 * HG : 3 * HG],
        channel_grads[KW + 1],
        grad_out_weight,
    )


def solution(mesh):
    in_specs = (
        P(("seq", "fsdp"), None),
        P(),
        P("fsdp", None),
        P(None, "seq", "fsdp"),
        P("seq", "fsdp"),
        P(),
        P(),
        P("seq"),
        P("seq"),
        P("seq"),
        P("seq", "fsdp"),
        P(None, "fsdp"),
        P(("seq", "fsdp"), None),
    )
    out_specs = (
        P(("seq", "fsdp"), None),
        P(("seq", "fsdp"), None),
        P(),
        P("fsdp", None),
        P(None, "seq", "fsdp"),
        P("seq", "fsdp"),
        P(),
        P(),
        P("seq"),
        P("seq"),
        P("seq"),
        P("seq", "fsdp"),
        P(None, "fsdp"),
    )
    return jax.shard_map(body, mesh=mesh, in_specs=in_specs, out_specs=out_specs, check_vma=False)
```

time: 2390 us -> 693 us (0.29)
  waiting for transfers between devices: 1280 us -> 183 us
  matrix products: 306 us -> 56.8 us
  other arithmetic: 317 us -> 130 us
  local copies, waits for them, and re-layouts: 316 us -> 157 us
  starting transfers between devices: 15.9 us -> 114 us
  blocking collectives: 122 us -> 39.7 us
    all_gather x3 -> x0, waiting for transfers between devices: 517 us -> none  [the longest x1 340 us: body(): lax.all_gather(in_weight, 'fsdp', axis=0, tiled=True)]
    unnamed x8 -> x0, waiting for transfers between devices: 484 us -> none
    dot_general x169 -> x26, matrix products: 306 us -> 56.8 us  [the longest x11 37.8 us: dot_f32(): lax.dot_general(left, right, (dims, batch), preferred_element_type=f32)]
    reduce_scatter x2 -> x0, waiting for transfers between devices: 181 us -> none  [the longest x1 140 us: body(): lax.psum_scatter(back_pair_raw, ('seq', 'fsdp'), scatter_dimension=1, til...]
    another operation x146 -> x9, other arithmetic: 184 us -> 9.41 us
    all_to_all x4 -> x25, waiting for transfers between devices: 45.7 us -> 179 us  [the longest x13 89.5 us: spread(): lax.all_to_all(copies, axis, 0, 0, axis_index_groups=groups, tiled=True)]
    psum x3 -> x0, blocking collectives: 122 us -> none  [the longest x1 42.4 us: body(): lax.psum((head_parts, pair_weight_part, pair_bias_part, gain_part), ('seq...]
    all_to_all x4 -> x25, starting transfers between devices: 15.4 us -> 107 us  [the longest x13 55.7 us: spread(): lax.all_to_all(copies, axis, 0, 0, axis_index_groups=groups, tiled=True)]
  transfers between devices with their start and end apart: 11 -> 37, of which waited for: 9 -> 22; matrix products, arithmetic and copies ran while one was open for 4% -> 39% of each run, Pallas kernels for 0% -> 0%
where the time goes in v1:
time: 693 us; the launch traced here: 684 us
  waiting for transfers between devices  183 us (26%)
  local copies, waits for them, and re-layouts  157 us (23%)
  other arithmetic  130 us (19%)
  starting transfers between devices  114 us (16%)
  matrix products  56.8 us (8%)
  blocking collectives  39.7 us (6%)
    all_to_all x13, waiting for transfers between devices, spread(): lax.all_to_all(copies, axis, 0, 0, axis_index_groups=groups, tiled=True)  89.5 us
    all_to_all x13, starting transfers between devices, spread(): lax.all_to_all(copies, axis, 0, 0, axis_index_groups=groups, tiled=True)  55.7 us
    all_to_all x1, blocking collectives, spread(): lax.all_to_all(copies, axis, 0, 0, axis_index_groups=groups, tiled=True)  39.7 us
    dot_general x11, matrix products, dot_f32(): lax.dot_general(left, right, (dims, batch), preferred_element_type=f32)  37.8 us
    all_to_all x3, waiting for transfers between devices, scatter_group(): got = lax.all_to_all(sent, 'fsdp', 0, 0, tiled=True)  34.5 us
    unnamed x219, local copies, waits for them, and re-layouts  26.6 us
    all_to_all x1, waiting for transfers between devices, body(): got = lax.all_to_all(sent, 'fsdp', 0, 0, tiled=True)  18.2 us
    broadcast_in_dim x17, local copies, waits for them, and re-layouts, spread(): copies = jnp.broadcast_to(value[None], (count,) + value.shape)  16.9 us
  transfers between devices with their start and end apart: 37, of which 22 were waited for; matrix products, arithmetic and copies ran while one was open for 39% of the time, Pallas kernels for 0%

profile of v1, /device:TPU:0, one launch (start us, length us, event | category | flops | bytes accessed | tf_op | source)
XLA Modules:
  0.0 683.5 jit_solution(1027061962513620722)
XLA Ops:
  4.7 7.3 %all-to-all-start = ((f32[32,8,128]{2,1,0:T(8,128)}), f32[32,8,128]{2,1,0:T(8,128)S(1)}, u32[]{:S(2)}, u32[]{:S(2)}) async-start(f32[32,8,128]{2,1,0:T(8,128)} %broadcast_in_dim.280), calls=%async_computation | async-start | bytes 262144 | tf_op jit(solution)/shard_map/all_to_all | solution.py:22
  12.9 5.0 fusion.150
  28.6 7.7 %all-to-all-done.6 = bf16[4,96,384]{2,1,0:T(8,128)(2,1)S(1)} async-done(((bf16[4,96,384]{2,1,0:T(8,128)(2,1)}), bf16[4,96,384]{2,1,0:T(8,128)(2,1)S(1)}, u32[]{:S(2)}, u32[]{:S(2)}) %all-to-all-start.6) | async-done | bytes 294944 | tf_op jit(solution)/shard_map/all_to_all | solution.py:150
  40.7 18.2 %all-to-all-done.2 = bf16[4,264,384]{2,1,0:T(8,128)(2,1)S(1)} async-done(((bf16[4,264,384]{2,1,0:T(8,128)(2,1)}), bf16[4,264,384]{2,1,0:T(8,128)(2,1)S(1)}, u32[]{:S(2)}, u32[]{:S(2)}) %all-to-all-start.2) | async-done | bytes 811040 | tf_op jit(solution)/shard_map/all_to_all | solution.py:134
  59.0 39.7 %all_to_all.130 = bf16[4,128,1536]{2,1,0:T(8,128)(2,1)} all-to-all(bf16[4,128,1536]{2,1,0:T(8,128)(2,1)S(1)} %broadcast_in_dim.281), channel_id=1, replica_groups=mesh['seq'=8,'fsdp'=4] {'fsdp'}, dimensions={0} | all-to-all | bytes 3145728 | tf_op jit(solution)/shard_map/all_to_all | solution.py:22
  103.6 35.8 %all-to-all-done.5 = bf16[4,128,1536]{2,1,0:T(8,128)(2,1)S(1)} async-done(((bf16[4,128,1536]{2,1,0:T(8,128)(2,1)}), bf16[4,128,1536]{2,1,0:T(8,128)(2,1)S(1)}, u32[]{:S(2)}, u32[]{:S(2)}) %all-to-all-start.5) | async-done | bytes 1572896 | tf_op jit(solution)/shard_map/all_to_all | solution.py:22
  164.7 17.4 %all-to-all-done.3 = bf16[4,264,1536]{2,1,0:T(8,128)(2,1)S(1)} async-done(((bf16[4,264,1536]{2,1,0:T(8,128)(2,1)}), bf16[4,264,1536]{2,1,0:T(8,128)(2,1)S(1)}, u32[]{:S(2)}, u32[]{:S(2)}) %all-to-all-start.3) | async-done | bytes 3244064 | tf_op jit(solution)/shard_map/all_to_all | solution.py:22
  266.0 6.0 multiply_reduce_fusion.8
  294.8 5.9 multiply_reduce_fusion.5
  340.6 5.0 multiply_reduce_fusion.6
  361.8 5.6 all-to-all-start.23
  375.8 8.0 %all-to-all-done.23 = bf16[4,96,1536]{2,1,0:T(8,128)(2,1)} async-done(((bf16[4,96,1536]{2,1,0:T(8,128)(2,1)}), bf16[4,96,1536]{2,1,0:T(8,128)(2,1)}, u32[]{:S(2)}, u32[]{:S(2)}) %all-to-all-start.23) | async-done | bytes 1179680 | tf_op jit(solution)/shard_map/all_to_all | solution.py:263
  390.8 6.9 %all-to-all-done.12 = bf16[4,128,256]{1,2,0:T(8,128)(2,1)S(1)} async-done(((bf16[4,128,256]{1,2,0:T(8,128)(2,1)}), bf16[4,128,256]{1,2,0:T(8,128)(2,1)S(1)}, u32[]{:S(2)}, u32[]{:S(2)}) %all-to-all-start.12) | async-done | bytes 262176 | tf_op jit(solution)/shard_map/all_to_all | solution.py:87
  422.9 5.1 all-to-all-start.24
  443.4 8.6 %all-to-all-done.18 = bf16[4,4,96,384]{3,2,1,0:T(8,128)(2,1)} async-done(((bf16[4,4,96,384]{3,2,1,0:T(8,128)(2,1)}), bf16[4,4,96,384]{3,2,1,0:T(8,128)(2,1)}, u32[]{:S(2)}, u32[]{:S(2)}) %all-to-all-start.18) | async-done | bytes 1179680 | tf_op jit(solution)/shard_map/all_to_all | solution.py:253
  459.8 7.3 %all-to-all-done.21 = bf16[4,160,256]{2,1,0:T(8,128)(2,1)S(1)} async-done(((bf16[4,160,256]{2,1,0:T(8,128)(2,1)}), bf16[4,160,256]{2,1,0:T(8,128)(2,1)S(1)}, u32[]{:S(2)}, u32[]{:S(2)}) %all-to-all-start.21) | async-done | bytes 327712 | tf_op jit(solution)/shard_map/all_to_all | solution.py:22
  472.1 6.2 all-to-all-done.19
  484.9 6.4 fusion.134
  491.5 5.4 all-to-all-done.17
  511.6 5.4 all-to-all-done.25
  521.7 8.1 %fusion.13 = f32[1024,1536]{1,0:T(8,128)} fusion(bf16[1024,6]{0,1:T(8,128)(2,1)} %copy-done.70, bf16[1024,384]{0,1:T(8,128)(2,1)S(1)} %slice.689, bf16[1024,384]{0,1:T(8,128)(2,1)} %get-tuple-element.143, bf16[8,1536]{1,0:T(8,128)(2,1)} %copy-done.80, bf16[384,1536]{1,0:T(8,128)(2,1)} %bitcast.350, bf16[384,1536]{1,0:T(8,128)(2,1)} %bitcast.348), kind=kOutput, calls=%fused_computation.64 | convolution fusion | flops 2454593536 | bytes 10260480 | tf_op jit(solution)/shard_map/dot_general | solution.py:26
  543.4 5.4 add_convert_fusion.1
  559.5 5.3 add_convert_fusion
  566.1 27.6 %all-to-all-done.9 = bf16[4,128,1536]{2,1,0:T(8,128)(2,1)S(1)} async-done(((bf16[4,128,1536]{2,1,0:T(8,128)(2,1)}), bf16[4,128,1536]{2,1,0:T(8,128)(2,1)S(1)}, u32[]{:S(2)}, u32[]{:S(2)}) %all-to-all-start.9) | async-done | bytes 1572896 | tf_op jit(solution)/shard_map/all_to_all | solution.py:87
  597.5 6.3 convert_bitcast_fusion.2
  603.9 6.4 reshape.857
  619.3 6.3 convert_bitcast_fusion.1
  625.6 6.4 reshape.858
  632.0 8.5 %pad_maximum_fusion = f32[384,6448]{1,0:T(8,128)} fusion(f32[384,304]{1,0:T(8,128)S(1)} %copy-done.34, f32[384,3072]{1,0:T(8,128)} %reshape.858, f32[384,3072]{1,0:T(8,128)} %reshape.857), kind=kLoop, calls=%fused_computation | loop fusion | flops 4952064 | bytes 19808256 | tf_op jit(solution)/shard_map/concatenate | solution.py:380
  640.6 10.7 %copy.363 = f32[384,6448]{0,1:T(8,128)} copy(f32[384,6448]{1,0:T(8,128)} %pad_maximum_fusion) | data formatting | bytes 19808256
  663.6 5.8 all-to-all-done.13
  676.1 5.1 all-to-all-done.14
  (535 shorter events, 365.6 us)
Async XLA Ops:
  4.7 16.7 %all-to-all-start = ((f32[32,8,128]{2,1,0:T(8,128)}), f32[32,8,128]{2,1,0:T(8,128)S(1)}, u32[]{:S(2)}, u32[]{:S(2)}) async-start(f32[32,8,128]{2,1,0:T(8,128)} %broadcast_in_dim.280), calls=%async_computation | async-start | bytes 262144 | tf_op jit(solution)/shard_map/all_to_all | solution.py:22
  21.5 14.8 %all-to-all-start.6 = ((bf16[4,96,384]{2,1,0:T(8,128)(2,1)}), bf16[4,96,384]{2,1,0:T(8,128)(2,1)S(1)}, u32[]{:S(2)}, u32[]{:S(2)}) async-start(bf16[4,96,384]{2,1,0:T(8,128)(2,1)} %dynamic-slice_bitcast_fusion), calls=%async_computation.6 | async-start | bytes 589824 | tf_op jit(solution)/shard_map/all_to_all | solution.py:150
  36.3 22.6 %all-to-all-start.2 = ((bf16[4,264,384]{2,1,0:T(8,128)(2,1)}), bf16[4,264,384]{2,1,0:T(8,128)(2,1)S(1)}, u32[]{:S(2)}, u32[]{:S(2)}) async-start(bf16[4,264,384]{2,1,0:T(8,128)(2,1)} %fusion.35), calls=%async_computation.2 | async-start | bytes 1622016 | tf_op jit(solution)/shard_map/all_to_all | solution.py:134
  100.0 39.5 %all-to-all-start.5 = ((bf16[4,128,1536]{2,1,0:T(8,128)(2,1)}), bf16[4,128,1536]{2,1,0:T(8,128)(2,1)S(1)}, u32[]{:S(2)}, u32[]{:S(2)}) async-start(bf16[4,128,1536]{2,1,0:T(8,128)(2,1)} %broadcast_in_dim.305), calls=%async_computation.5 | async-start | bytes 3145728 | tf_op jit(solution)/shard_map/all_to_all | solution.py:22
  141.7 40.4 %all-to-all-start.3 = ((bf16[4,264,1536]{2,1,0:T(8,128)(2,1)}), bf16[4,264,1536]{2,1,0:T(8,128)(2,1)S(1)}, u32[]{:S(2)}, u32[]{:S(2)}) async-start(bf16[4,264,1536]{2,1,0:T(8,128)(2,1)} %broadcast_in_dim.285), calls=%async_computation.3 | async-start | bytes 6488064 | tf_op jit(solution)/shard_map/all_to_all | solution.py:22
  158.8 23.7 %collective-permute-start = (bf16[4,128,1536]{2,1,0:T(8,128)(2,1)}, bf16[4,128,1536]{2,1,0:T(8,128)(2,1)}, u32[]{:S(2)}, u32[]{:S(2)}) collective-permute-start(bf16[4,128,1536]{2,1,0:T(8,128)(2,1)} %all_to_all.130), channel_id=1, source_target_pairs={{0,4},{4,0},{8,12},{12,8},{16,20},{20,16},{24,28},{28,24},{1,5},{5... | collective-permute-start | bytes 4718600 | tf_op jit(solution)/shard_map/ppermute | solution.py:69
  164.2 33.7 %collective-permute-start.2 = (bf16[4,128,1536]{2,1,0:T(8,128)(2,1)}, bf16[4,128,1536]{2,1,0:T(8,128)(2,1)}, u32[]{:S(2)}, u32[]{:S(2)}) collective-permute-start(bf16[4,128,1536]{2,1,0:T(8,128)(2,1)} %copy-done.20), channel_id=1, source_target_pairs={{0,4},{4,0},{8,12},{12,8},{16,20},{20,16},{24,28},{28,24},{1,5},{5... | collective-permute-start | bytes 4718600 | tf_op jit(solution)/shard_map/ppermute | solution.py:69
  192.0 18.9 %collective-permute-start.1 = (bf16[3,640]{0,1:T(8,128)(2,1)S(1)}, bf16[3,640]{0,1:T(8,128)(2,1)}, u32[]{:S(2)}, u32[]{:S(2)}) collective-permute-start(bf16[3,640]{0,1:T(8,128)(2,1)S(1)} %pad_maximum_fusion.9), channel_id=1, source_target_pairs={{0,8},{4,12},{8,16},{12,20},{16,24},{20,28},{1,9},{5,13},{9,17},{1... | collective-permute-start | bytes 11528 | tf_op jit(solution)/shard_map/ppermute | solution.py:164
  230.8 14.0 %all-to-all-start.4 = ((f32[4,136,384]{2,1,0:T(8,128)}), f32[4,136,384]{2,1,0:T(8,128)}, u32[]{:S(2)}, u32[]{:S(2)}) async-start(f32[4,136,384]{2,1,0:T(8,128)} %broadcast_in_dim.297), calls=%async_computation.4 | async-start | bytes 1671168 | tf_op jit(solution)/shard_map/all_to_all | solution.py:22
  246.9 19.1 %all-to-all-start.7 = ((bf16[4,96,1536]{2,1,0:T(8,128)(2,1)}), bf16[4,96,1536]{2,1,0:T(8,128)(2,1)}, u32[]{:S(2)}, u32[]{:S(2)}) async-start(bf16[4,96,1536]{2,1,0:T(8,128)(2,1)} %broadcast_in_dim.307), calls=%async_computation.7 | async-start | bytes 2359296 | tf_op jit(solution)/shard_map/all_to_all | solution.py:22
  273.9 18.8 %all-to-all-start.8 = ((f32[4,2,1024]{2,1,0:T(2,128)}), f32[4,2,1024]{2,1,0:T(2,128)}, u32[]{:S(2)}, u32[]{:S(2)}) async-start(f32[4,2,1024]{2,1,0:T(2,128)} %broadcast_in_dim.308), calls=%async_computation.8 | async-start | bytes 65536 | tf_op jit(solution)/shard_map/all_to_all | solution.py:22
  311.6 20.0 %all-to-all-start.10 = ((f32[4,128,384]{2,1,0:T(8,128)}), f32[4,128,384]{2,1,0:T(8,128)}, u32[]{:S(2)}, u32[]{:S(2)}) async-start(f32[4,128,384]{2,1,0:T(8,128)} %broadcast_in_dim.311), calls=%async_computation.10 | async-start | bytes 1572864 | tf_op jit(solution)/shard_map/all_to_all | solution.py:22
  331.6 30.3 %all-to-all-start.15 = ((bf16[4,4,96,384]{3,2,1,0:T(8,128)(2,1)}), bf16[4,4,96,384]{3,2,1,0:T(8,128)(2,1)}, u32[]{:S(2)}, u32[]{:S(2)}) async-start(bf16[4,4,96,384]{3,2,1,0:T(8,128)(2,1)} %bitcast.327), calls=%async_computation.15 | async-start | bytes 2359296 | tf_op jit(solution)/shard_map/all_to_all | solution.py:253
  361.8 22.0 %all-to-all-start.23 = ((bf16[4,96,1536]{2,1,0:T(8,128)(2,1)}), bf16[4,96,1536]{2,1,0:T(8,128)(2,1)}, u32[]{:S(2)}, u32[]{:S(2)}) async-start(bf16[4,96,1536]{2,1,0:T(8,128)(2,1)} %bitcast.341), calls=%async_computation.23 | async-start | bytes 2359296 | tf_op jit(solution)/shard_map/all_to_all | solution.py:263
  383.8 13.9 %all-to-all-start.12 = ((bf16[4,128,256]{1,2,0:T(8,128)(2,1)}), bf16[4,128,256]{1,2,0:T(8,128)(2,1)S(1)}, u32[]{:S(2)}, u32[]{:S(2)}) async-start(bf16[4,128,256]{1,2,0:T(8,128)(2,1)} %copy_bitcast_fusion.2), calls=%async_computation.12 | async-start | bytes 524288 | tf_op jit(solution)/shard_map/all_to_all | solution.py:87
  398.4 24.5 %all-to-all-start.16 = ((bf16[4,96,384]{2,1,0:T(8,128)(2,1)}), bf16[4,96,384]{2,1,0:T(8,128)(2,1)S(1)}, u32[]{:S(2)}, u32[]{:S(2)}) async-start(bf16[4,96,384]{2,1,0:T(8,128)(2,1)} %reduce_sum.394), calls=%async_computation.16 | async-start | bytes 589824 | tf_op jit(solution)/shard_map/all_to_all | solution.py:257
  422.9 12.1 %all-to-all-start.24 = ((bf16[4,96,384]{2,1,0:T(8,128)(2,1)}), bf16[4,96,384]{2,1,0:T(8,128)(2,1)S(1)}, u32[]{:S(2)}, u32[]{:S(2)}) async-start(bf16[4,96,384]{2,1,0:T(8,128)(2,1)} %copy.360), calls=%async_computation.24 | async-start | bytes 589824 | tf_op jit(solution)/shard_map/all_to_all | solution.py:272
  435.0 17.0 %all-to-all-start.18 = ((bf16[4,4,96,384]{3,2,1,0:T(8,128)(2,1)}), bf16[4,4,96,384]{3,2,1,0:T(8,128)(2,1)}, u32[]{:S(2)}, u32[]{:S(2)}) async-start(bf16[4,4,96,384]{3,2,1,0:T(8,128)(2,1)} %bitcast.328), calls=%async_computation.18 | async-start | bytes 2359296 | tf_op jit(solution)/shard_map/all_to_all | solution.py:253
  452.8 14.3 %all-to-all-start.21 = ((bf16[4,160,256]{2,1,0:T(8,128)(2,1)}), bf16[4,160,256]{2,1,0:T(8,128)(2,1)S(1)}, u32[]{:S(2)}, u32[]{:S(2)}) async-start(bf16[4,160,256]{2,1,0:T(8,128)(2,1)} %broadcast_in_dim.326), calls=%async_computation.21 | async-start | bytes 655360 | tf_op jit(solution)/shard_map/all_to_all | solution.py:22
  480.6 16.4 %all-to-all-start.17 = ((bf16[4,4,96,384]{3,1,2,0:T(4,128)(2,1)}), bf16[4,4,96,384]{3,1,2,0:T(4,128)(2,1)}, u32[]{:S(2)}, u32[]{:S(2)}) async-start(bf16[4,4,96,384]{3,1,2,0:T(4,128)(2,1)} %broadcast_in_dim.324), calls=%async_computation.17 | async-start | bytes 2359296 | tf_op jit(solution)/shard_map/all_to_all | solution.py:22
  491.5 15.7 %collective-permute-start.10 = (bf16[4,160,256]{2,1,0:T(8,128)(2,1)S(1)}, bf16[4,160,256]{2,1,0:T(8,128)(2,1)}, u32[]{:S(2)}, u32[]{:S(2)}) collective-permute-start(bf16[4,160,256]{2,1,0:T(8,128)(2,1)S(1)} %all-to-all-done.21), channel_id=1, source_target_pairs={{0,4},{4,0},{8,12},{12,8},{16,20},{20,16},{24,28},{28,24},{1,5},{5... | collective-permute-start | bytes 983048 | tf_op jit(solution)/shard_map/ppermute | solution.py:69
  498.3 18.7 %all-to-all-start.25 = ((bf16[4,4,96,384]{3,1,2,0:T(4,128)(2,1)}), bf16[4,4,96,384]{3,1,2,0:T(4,128)(2,1)}, u32[]{:S(2)}, u32[]{:S(2)}) async-start(bf16[4,4,96,384]{3,1,2,0:T(4,128)(2,1)} %broadcast_in_dim.328), calls=%async_computation.25 | async-start | bytes 2359296 | tf_op jit(solution)/shard_map/all_to_all | solution.py:22
  507.2 36.2 %collective-permute-start.4 = (bf16[512,1536]{1,0:T(8,128)(2,1)}, bf16[512,1536]{1,0:T(8,128)(2,1)}, u32[]{:S(2)}, u32[]{:S(2)}) collective-permute-start(bf16[512,1536]{1,0:T(8,128)(2,1)} %select_convert_fusion.1), channel_id=1, source_target_pairs={{0,4},{4,0},{8,12},{12,8},{16,20},{20,16},{24,28},{28,24},{1,5},{5... | collective-permute-start | bytes 4718600 | tf_op jit(solution)/shard_map/ppermute | solution.py:69
  518.0 15.4 %all-to-all-start.22 = ((bf16[4,304,384]{2,1,0:T(8,128)(2,1)}), bf16[4,304,384]{2,1,0:T(8,128)(2,1)S(1)}, u32[]{:S(2)}, u32[]{:S(2)}) async-start(bf16[4,304,384]{2,1,0:T(8,128)(2,1)} %broadcast_in_dim.327), calls=%async_computation.22 | async-start | bytes 1867776 | tf_op jit(solution)/shard_map/all_to_all | solution.py:22
  534.8 18.9 %all-to-all-start.20 = ((bf16[4,4,96,384]{3,1,2,0:T(4,128)(2,1)}), bf16[4,4,96,384]{3,1,2,0:T(4,128)(2,1)}, u32[]{:S(2)}, u32[]{:S(2)}) async-start(bf16[4,4,96,384]{3,1,2,0:T(4,128)(2,1)} %broadcast_in_dim.325), calls=%async_computation.20 | async-start | bytes 2359296 | tf_op jit(solution)/shard_map/all_to_all | solution.py:22
  543.4 16.2 %collective-permute-start.6 = (bf16[512,1536]{1,0:T(8,128)(2,1)}, bf16[512,1536]{1,0:T(8,128)(2,1)}, u32[]{:S(2)}, u32[]{:S(2)}) collective-permute-start(bf16[512,1536]{1,0:T(8,128)(2,1)} %select_convert_fusion), channel_id=1, source_target_pairs={{0,4},{4,0},{8,12},{12,8},{16,20},{20,16},{24,28},{28,24},{1,5},{5... | collective-permute-start | bytes 4718600 | tf_op jit(solution)/shard_map/ppermute | solution.py:69
  553.7 40.0 %all-to-all-start.9 = ((bf16[4,128,1536]{2,1,0:T(8,128)(2,1)}), bf16[4,128,1536]{2,1,0:T(8,128)(2,1)S(1)}, u32[]{:S(2)}, u32[]{:S(2)}) async-start(bf16[4,128,1536]{2,1,0:T(8,128)(2,1)} %bitcast.51), calls=%async_computation.9 | async-start | bytes 3145728 | tf_op jit(solution)/shard_map/all_to_all | solution.py:87
  558.0 39.6 %collective-permute-start.8 = (bf16[4,4,96,384]{3,1,2,0:T(4,128)(2,1)}, bf16[4,4,96,384]{3,1,2,0:T(4,128)(2,1)}, u32[]{:S(2)}, u32[]{:S(2)}) collective-permute-start(bf16[4,4,96,384]{3,1,2,0:T(4,128)(2,1)} %all-to-all-done.17), channel_id=1, source_target_pairs={{0,4},{4,0},{8,12},{12,8},{16,20},{20,16},{24,28},{28,24},{1,5},{5... | collective-permute-start | bytes 3538952 | tf_op jit(solution)/shard_map/ppermute | solution.py:69
  559.0 51.3 %collective-permute-start.11 = (bf16[4,4,96,384]{3,1,2,0:T(4,128)(2,1)}, bf16[4,4,96,384]{3,1,2,0:T(4,128)(2,1)}, u32[]{:S(2)}, u32[]{:S(2)}) collective-permute-start(bf16[4,4,96,384]{3,1,2,0:T(4,128)(2,1)} %all-to-all-done.25), channel_id=1, source_target_pairs={{0,4},{4,0},{8,12},{12,8},{16,20},{20,16},{24,28},{28,24},{1,5},{5... | collective-permute-start | bytes 3538952 | tf_op jit(solution)/shard_map/ppermute | solution.py:69
  564.9 54.4 %collective-permute-start.9 = (bf16[4,4,96,384]{3,1,2,0:T(4,128)(2,1)}, bf16[4,4,96,384]{3,1,2,0:T(4,128)(2,1)}, u32[]{:S(2)}, u32[]{:S(2)}) collective-permute-start(bf16[4,4,96,384]{3,1,2,0:T(4,128)(2,1)} %all-to-all-done.20), channel_id=1, source_target_pairs={{0,4},{4,0},{8,12},{12,8},{16,20},{20,16},{24,28},{28,24},{1,5},{5... | collective-permute-start | bytes 3538952 | tf_op jit(solution)/shard_map/ppermute | solution.py:69
  593.7 57.5 %all-to-all-start.11 = ((bf16[4,128,1536]{2,1,0:T(8,128)(2,1)}), bf16[4,128,1536]{2,1,0:T(8,128)(2,1)S(1)}, u32[]{:S(2)}, u32[]{:S(2)}) async-start(bf16[4,128,1536]{2,1,0:T(8,128)(2,1)} %bitcast.77), calls=%async_computation.11 | async-start | bytes 3145728 | tf_op jit(solution)/shard_map/all_to_all | solution.py:87
  656.6 12.7 %all-to-all-start.13 = ((f32[32,8,128]{2,1,0:T(8,128)}), f32[32,8,128]{2,1,0:T(8,128)}, u32[]{:S(2)}, u32[]{:S(2)}) async-start(f32[32,8,128]{2,1,0:T(8,128)} %pad_maximum_fusion.10), calls=%async_computation.13 | async-start | bytes 262144 | tf_op jit(solution)/shard_map/all_to_all | solution.py:409
  (112 other events, 865.8 us)
